TPU v7x, 768 devices: a whole 4x8x12 slice. The times are simulated.
768 devices in a mesh: space: 192 (over z, y, x_hi), cuts: 4 (over x_lo, core).
Axes of the slice: x: 4 (x_hi: 2, x_lo: 2; x = x_hi * 2 + x_lo), y: 8, z: 12, core: 2. Of those that a mesh axis runs over, the one named last changes fastest.
Arguments:
- vectors: float32 [4, 2, 512, 49152], P('cuts', None, None, 'space'), may hold values from -0.75 to 0.75
- momenta: int32 [3, 3], replicated, may hold values from -3 to 3, as said below
- diagrams: int32 [64, 5], replicated, may hold values from 0 to 3, as said below
Outputs:
- meson: float32 [4, 1536, 1024], P('cuts', 'space')
- diagram_values: float32 [64, 2], replicated
Inputs may be any that keep to these rules, and one draw needn't show every extreme that they name: `momenta`: first component of each momentum is nonzero. `diagrams`: column 0 is a tile id below (2)**2, columns 1 and 2 are time slices, column 3 a phase, column 4 the owner index along cuts; no owner is named more than 32 times and one owner exactly 32 times.
All inputs are finite; a program needn't handle non-finite values.
Results may differ from a plain program's by a relative error of at most 0.0003.
Values sent between devices are 32-bit elements; how exact they have to be, the bound alone decides.
A program may use at most 32 MiB of HBM per device.

v0:
```python
import math

import jax
import jax.numpy as jnp
from jax import lax
from jax.sharding import PartitionSpec as P

MODES = 512
TILE = 256
PHASES = 3
EXTENT = 96


full_turn = 2.0 * math.pi


def angles_for(moment_rows, site_ids):
    coord_x = site_ids % EXTENT
    coord_y = site_ids // EXTENT % EXTENT
    coord_z = site_ids // (EXTENT * EXTENT)
    dotted = (
        moment_rows[:, 0:1] * coord_x[None, :]
        + moment_rows[:, 1:2] * coord_y[None, :]
        + moment_rows[:, 2:3] * coord_z[None, :]
    )
    return jnp.mod(dotted, EXTENT).astype(jnp.float32) * (full_turn / EXTENT)


def phased_rows(real_vec, imag_vec, moment_rows, site_ids):
    angle = angles_for(moment_rows, site_ids)
    cosine = jnp.cos(angle)
    sine = jnp.sin(angle)
    left_real = real_vec * cosine + imag_vec * sine
    left_imag = real_vec * sine - imag_vec * cosine
    return jnp.concatenate([left_real, left_imag], axis=1)


def right_block(real_vec, imag_vec):
    upper = jnp.concatenate([real_vec, -imag_vec], axis=1)
    lower = jnp.concatenate([imag_vec, real_vec], axis=1)
    return jnp.concatenate([upper, lower], axis=0)


def contract(left, right):
    return lax.dot_general(
        left,
        right,
        (((1,), (1,)), ((), ())),
        precision=lax.Precision.HIGHEST,
        preferred_element_type=jnp.float32,
    )


def tile_columns(rows, column_start):
    real_cols = lax.dynamic_slice_in_dim(rows, column_start, TILE, 1)
    imag_cols = lax.dynamic_slice_in_dim(rows, column_start + MODES, TILE, 1)
    return (real_cols, imag_cols)


def tile_pair(first_real, first_imag, second_real, second_imag, mask):
    real_rows = jnp.sum(first_real * second_real + first_imag * second_imag, axis=1)
    imag_rows = jnp.sum(first_imag * second_real - first_real * second_imag, axis=1)
    return jnp.stack([jnp.sum(mask * real_rows), jnp.sum(mask * imag_rows)]) / TILE


def per_device(vectors, momenta, diagrams):
    real_vec = vectors[0, 0]
    imag_vec = vectors[0, 1]
    sites_dev = real_vec.shape[1]
    site_ids = lax.axis_index("space") * sites_dev + jnp.arange(sites_dev, dtype=jnp.int32)
    right = right_block(real_vec, imag_vec)
    own_rows = PHASES * MODES // lax.axis_size("space")
    row_ids = jnp.arange(lax.axis_size("space") * own_rows, dtype=jnp.int32)
    mode_ids = row_ids % MODES
    phase_ids = row_ids // MODES
    field_rows = lax.psum_scatter(
        contract(
            phased_rows(
                jnp.take(real_vec, mode_ids, axis=0),
                jnp.take(imag_vec, mode_ids, axis=0),
                jnp.take(momenta, phase_ids, axis=0),
                site_ids,
            ),
            right,
        ),
        "space",
        scatter_dimension=0,
        tiled=True,
    )
    global_rows = lax.axis_index("space") * own_rows + jnp.arange(own_rows, dtype=jnp.int32)
    tiles_per = MODES // TILE

    def row_mask(entry):
        row_start = entry[3] * MODES + entry[0] // tiles_per * TILE
        return ((global_rows >= row_start) & (global_rows < row_start + TILE)).astype(jnp.float32)

    all_slices = lax.all_gather(field_rows[None], "cuts", axis=0, tiled=True)

    def one_product(entry):
        column_start = entry[0] % tiles_per * TILE
        first = lax.dynamic_index_in_dim(all_slices, entry[1], 0, keepdims=False)
        second = lax.dynamic_index_in_dim(all_slices, entry[2], 0, keepdims=False)
        first_real, first_imag = tile_columns(first, column_start)
        second_real, second_imag = tile_columns(second, column_start)
        return tile_pair(first_real, first_imag, second_real, second_imag, row_mask(entry))

    partial_value = lax.map(one_product, diagrams)
    totals = lax.psum(partial_value, "space")
    return (field_rows[None], totals)


def solution(mesh):
    placed = (P("cuts", None, None, "space"), P(), P())
    return jax.shard_map(
        per_device,
        mesh=mesh,
        in_specs=placed,
        out_specs=(P("cuts", "space", None), P()),
        check_vma=False,
    )
```

profile of v0, /device:TPU:2, one launch (start us, length us, event | category | flops | bytes accessed | tf_op | source)
XLA Modules:
  0.0 2305.6 jit_solution(12301692720325304445)
XLA Ops:
  7.4 1.4 slice_bitcast_fusion.1
  9.6 3.7 gather_fusion.1
  13.3 4.7 gather_fusion.2
  18.0 2.6 gather_fusion
  22.3 7.5 multiply_add_fusion
  29.8 12.1 fusion.2
  42.0 1089.5 %reduce-scatter.2.cloned.1.call-done = f32[8,1024]{1,0:T(8,128)} async-done(((f32[1536,1024]{1,0:T(8,128)}), f32[8,1024]{1,0:T(8,128)}) %reduce-scatter.2.cloned.1.call-update) | async-done | bytes 32784 | tf_op jit(solution)/shard_map/reduce_scatter | solution.py:76
  1131.4 5.6 all-gather
  1137.1 632.9 %while.14 = (s32[]{:T(128)}, f32[64,2]{0,1:T(2,128)S(1)}, s32[64,5]{0,1:T(8,128)S(1)}, f32[4,8,1024]{2,1,0:T(8,128)S(1)}, s32[]{:T(128)}, /*index=5*/s32[]{:T(12...) while((s32[]{:T(128)}, f32[64,2]{0,1:T(2,128)S(1)}, ...), condition=%wide.region_6.8_spmd.clone, body=%wide.region_1.0_spmd.clone.sunk | while | flops 16477 | bytes 33660 | solution.py:107
  1145.6 1.3 maximum_multiply_fusion.2
  1165.3 1.3 maximum_multiply_fusion.2
  1175.2 1.3 maximum_multiply_fusion.2
  1185.1 1.3 maximum_multiply_fusion.2
  1195.0 1.3 maximum_multiply_fusion.2
  1204.9 1.3 maximum_multiply_fusion.2
  1214.7 1.3 maximum_multiply_fusion.2
  1224.6 1.3 maximum_multiply_fusion.2
  1234.5 1.3 maximum_multiply_fusion.2
  1244.4 1.3 maximum_multiply_fusion.2
  1254.3 1.3 maximum_multiply_fusion.2
  1264.2 1.3 maximum_multiply_fusion.2
  1274.1 1.3 maximum_multiply_fusion.2
  1293.9 1.3 maximum_multiply_fusion.2
  1303.7 1.3 maximum_multiply_fusion.2
  1323.5 1.3 maximum_multiply_fusion.2
  1333.4 1.3 maximum_multiply_fusion.2
  1353.2 1.3 maximum_multiply_fusion.2
  1363.1 1.3 maximum_multiply_fusion.2
  1373.0 1.3 maximum_multiply_fusion.2
  1382.9 1.3 maximum_multiply_fusion.2
  1392.8 1.3 maximum_multiply_fusion.2
  1402.6 1.3 maximum_multiply_fusion.2
  1412.5 1.3 maximum_multiply_fusion.2
  1422.4 1.3 maximum_multiply_fusion.2
  1432.3 1.3 maximum_multiply_fusion.2
  1442.2 1.3 maximum_multiply_fusion.2
  1452.1 1.3 maximum_multiply_fusion.2
  1462.0 1.3 maximum_multiply_fusion.2
  1481.8 1.3 maximum_multiply_fusion.2
  1491.6 1.3 maximum_multiply_fusion.2
  1511.4 1.3 maximum_multiply_fusion.2
  1521.3 1.3 maximum_multiply_fusion.2
  1541.1 1.3 maximum_multiply_fusion.2
  1551.0 1.3 maximum_multiply_fusion.2
  1560.9 1.3 maximum_multiply_fusion.2
  1570.8 1.3 maximum_multiply_fusion.2
  1580.7 1.3 maximum_multiply_fusion.2
  1590.5 1.3 maximum_multiply_fusion.2
  1600.4 1.3 maximum_multiply_fusion.2
  1610.3 1.3 maximum_multiply_fusion.2
  1620.2 1.3 maximum_multiply_fusion.2
  1630.1 1.3 maximum_multiply_fusion.2
  1640.0 1.3 maximum_multiply_fusion.2
  1649.9 1.3 maximum_multiply_fusion.2
  1669.7 1.3 maximum_multiply_fusion.2
  1679.5 1.3 maximum_multiply_fusion.2
  1699.3 1.3 maximum_multiply_fusion.2
  1709.2 1.3 maximum_multiply_fusion.2
  1729.0 1.3 maximum_multiply_fusion.2
  1738.9 1.3 maximum_multiply_fusion.2
  1748.8 1.3 maximum_multiply_fusion.2
  1758.7 1.3 maximum_multiply_fusion.2
  1768.6 1.3 maximum_multiply_fusion.2
  1769.9 528.8 %psum.7 = f32[64,2]{0,1:T(2,128)} all-reduce(f32[64,2]{0,1:T(2,128)S(1)} %get-tuple-element.105), channel_id=1, replica_groups=mesh['space'=192,'cuts'=4] {'space'}, use_global_device_ids=true, to_apply=%region_7.9 | all-reduce | flops 128 | bytes 1024 | tf_op jit(solution)/shard_map/psum | solution.py:108
  (354 shorter events, 122.6 us)
Async XLA Ops:
  7.2 10.8 copy-start
  7.2 1.6 copy-start.2
  7.2 1124.2 %reduce-scatter.2.cloned.1.call-start = ((), (), s32[]{:S(2)}) async-start(), calls=%async_computation.1 | async-start | bytes 6324224 | tf_op jit(solution)/shard_map/reduce_scatter | solution.py:76
  20.9 1.4 copy-start.1
  22.3 7.5 copy-start.3
  41.9 1095.1 %copy-start.4 = (s32[64,5]{0,1:T(8,128)S(1)}, s32[64,5]{0,1:T(8,128)}, u32[]{:S(2)}) copy-start(s32[64,5]{0,1:T(8,128)} %param.9) | copy-start | bytes 3844
Sparse Core Ops, SparseCore 0:
  42.1 1089.2 reduce-scatter.1
where the time goes:
time: 2310 us
  waiting for transfers between devices  1090 us (47%)
  blocking collectives  534 us (23%)
  loops' own time  445 us (19%)
  other arithmetic  146 us (6%)
  local copies, waits for them, and re-layouts  64.1 us (3%)
    reduce_scatter x1, waiting for transfers between devices, per_device(): lax.psum_scatter(contract(phased_rows(jnp.take(real_vec, mode_ids, axis=0...  1090 us
    psum x1, blocking collectives, per_device(): totals = lax.psum(partial_value, 'space')  529 us
    another operation x1, loops' own time, per_device(): partial_value = lax.map(one_product, diagrams)  445 us
    div x64, other arithmetic, tile_pair(): jnp.stack([jnp.sum(mask * real_rows), jnp.sum(mask * imag_rows)]) / TILE  80.3 us
  transfers between devices with their start and end apart: 1, of which 1 were waited for; matrix products, arithmetic and copies ran while one was open for 0% of the time, Pallas kernels for 0%

commit v1 on v0

v1 whole, which is shorter than its diff:
```python
import functools
import math

import jax
import jax.numpy as jnp
from jax import lax
from jax.experimental import pallas as pl
from jax.experimental.pallas import tpu as pltpu
from jax.sharding import PartitionSpec as P

TILE = 256
PHASES = 3
EXTENT = 96
RINGS = (12, 8, 2)
CUTS = 4
SUBS = 2
HOP_Z, HOP_Y, HOP_SMALL = 2.6, 3.9, 1.6

full_turn = 2.0 * math.pi
MESH = pl.DeviceIdType.MESH


def contract(left, right):
    return lax.dot_general(
        left, right, (((1,), (1,)), ((), ())), preferred_element_type=jnp.float32
    )


def halves(value):
    high = value.astype(jnp.bfloat16)
    low = (value - high.astype(jnp.float32)).astype(jnp.bfloat16)
    return high, low


class Ring:
    def __init__(self, name, extent, hop):
        self.name, self.extent, self.hop = name, extent, hop
        self.hops = (extent // 2, extent - 1 - extent // 2)


def kernel(
    vec_ref,
    mom_ref,
    dia_ref,
    meson_ref,
    value_ref,
    left,
    right,
    a0,
    a1,
    b0,
    b1,
    own_a,
    own_b,
    c0,
    c1,
    d0,
    d1,
    piece,
    got,
    whole,
    total,
    sum_y,
    sum_x,
    sum_z,
    send_a,
    recv_a,
    send_b,
    recv_b,
    send_c,
    recv_c,
    send_d,
    recv_d,
    send_e,
    recv_e,
    send_y,
    recv_y,
    send_x,
    recv_x,
    send_z,
    recv_z,
):
    nz, ny, nx = RINGS
    nc = CUTS
    modes, sites = vec_ref.shape[2:]
    width = modes // SUBS
    rows_y = left.shape[2]
    rows_z = ny * rows_y
    rows_x = rows_y // nx
    quarter = modes // nc
    space = lax.axis_index("space")
    cut = lax.axis_index("cuts")
    x = lax.rem(space, nx)
    y = lax.rem(space // nx, ny)
    z = space // (nx * ny)
    sign = 1 - 2 * lax.rem(cut, 2)

    def at(zz, yy, xx, cc):
        return ((zz * ny + yy) * nx + xx, cc)

    def z_at(step):
        return lax.rem(z + step + 2 * nz, nz)

    def y_at(step):
        return lax.rem(y + step + 2 * ny, ny)

    peers = [at(z_at(k), y, x, cut) for k in range(1, nz)]
    peers += [at(z, y_at(k), x, cut) for k in range(1, ny)]
    others = [
        (lax.rem(x + dx, nx), lax.rem(cut + dc, nc), dx, dc)
        for dx in range(nx)
        for dc in range(nc)
        if dx or dc
    ]
    peers += [at(z, y, xx, cc) for xx, cc, _, _ in others]
    barrier = pltpu.get_barrier_semaphore()
    for peer in peers:
        pl.semaphore_signal(barrier, inc=1, device_id=peer, device_id_type=MESH)

    real_vec = vec_ref[0, 0]
    imag_vec = vec_ref[0, 1]
    depth = 2 * sites
    rh, rl = halves(real_vec)
    ih, il = halves(imag_vec)
    for part, (first, second) in enumerate((((rh, rl), (-ih, -il)), ((ih, il), (rh, rl)))):
        rows = slice(part * modes, (part + 1) * modes)
        for place, (high, low) in enumerate((first, second)):
            cols = place * sites
            right[rows, cols : cols + sites] = high
            right[rows, depth + cols : depth + cols + sites] = high
            right[rows, 2 * depth + cols : 2 * depth + cols + sites] = low

    lane = lax.broadcasted_iota(jnp.int32, (1, sites), 1)
    site = (space * sites + lane).astype(jnp.float32)
    line = jnp.floor((site + 0.5) * (1.0 / EXTENT))
    coord_x = site - line * EXTENT
    coord_z = jnp.floor((line + 0.5) * (1.0 / EXTENT))
    coord_y = line - coord_z * EXTENT
    blocks = modes // rows_y
    for phase in range(PHASES):
        dotted = (
            mom_ref[phase, 0].astype(jnp.float32) * coord_x
            + mom_ref[phase, 1].astype(jnp.float32) * coord_y
            + mom_ref[phase, 2].astype(jnp.float32) * coord_z
        )
        turned = dotted - jnp.floor((dotted + 0.5) * (1.0 / EXTENT)) * EXTENT
        angle = turned * (full_turn / EXTENT)
        cosine = jnp.cos(angle)
        sine = jnp.sin(angle)
        for place, value in enumerate(
            (real_vec * cosine + imag_vec * sine, real_vec * sine - imag_vec * cosine)
        ):
            high, low = halves(value)
            cols = place * sites
            for block in range(blocks):
                zz, yy = divmod(phase * blocks + block, ny)
                rows = slice(block * rows_y, (block + 1) * rows_y)
                left[zz, yy, :, cols : cols + sites] = high[rows]
                left[zz, yy, :, depth + cols : depth + cols + sites] = low[rows]
                left[zz, yy, :, 2 * depth + cols : 2 * depth + cols + sites] = high[rows]

    pl.semaphore_wait(barrier, len(peers))
    sends = []

    def post(source, target, send_sem, recv_sem, peer):
        copy = pltpu.make_async_remote_copy(
            src_ref=source,
            dst_ref=target,
            send_sem=send_sem,
            recv_sem=recv_sem,
            device_id=peer,
            device_id_type=MESH,
        )
        copy.start()
        sends.append(copy)

    def arrived(target, send_sem, recv_sem):
        pltpu.make_async_remote_copy(
            src_ref=target,
            dst_ref=target,
            send_sem=send_sem,
            recv_sem=recv_sem,
            device_id=at(z, y, x, cut),
            device_id_type=MESH,
        ).wait_recv()

    def local_a(zz, sub):
        rows = left[zz].reshape(rows_z, left.shape[3])
        return contract(rows, right[sub * width : (sub + 1) * width, :])

    def local_b(yy, sub):
        rows = left[:, yy].reshape(nz * rows_y, left.shape[3])
        start = modes + sub * width
        return contract(rows, right[start : start + width, :])

    def ring(ring_of, slots, send_sems, recv_sems, sub, local, finish, step_at, peer_of, start, tick):
        hops = ring_of.hops

        def hop(direction, step):
            way = sign if direction == 0 else -sign
            buffer = slots[direction]
            here = buffer.at[step, sub]
            if step:
                mine = local(step_at(way * (hops[direction] - step)), sub)
                arrived(here, send_sems.at[direction, step - 1, sub], recv_sems.at[direction, step - 1, sub])
                here[...] += mine
            else:
                here[...] = local(step_at(way * hops[direction]), sub)
            post(
                here,
                buffer.at[step + 1, sub],
                send_sems.at[direction, step, sub],
                recv_sems.at[direction, step, sub],
                peer_of(way),
            )

        def last():
            value = local(step_at(0), sub)
            for direction in (0, 1):
                count = hops[direction]
                if count:
                    here = slots[direction].at[count, sub]
                    arrived(here, send_sems.at[direction, count - 1, sub], recv_sems.at[direction, count - 1, sub])
                    value += here[...]
            finish(sub, value)

        for direction in (0, 1):
            for step in range(hops[direction]):
                yield start + tick * (step * SUBS + sub), functools.partial(hop, direction, step)
        yield start + tick * (hops[0] * SUBS + sub), last

    def z_peer(way):
        return at(z_at(way), y, x, cut)

    def y_peer(way):
        return at(z, y_at(way), x, cut)

    ring_z = Ring("z", nz, HOP_Z)
    ring_y = Ring("y", ny, HOP_Y)

    def keep_a(sub, value):
        own_a[sub] = value.reshape(ny, rows_y, width)

    def keep_b(sub, value):
        own_b[sub] = value.reshape(nz, rows_y, width)

    per = width // quarter

    def keep_piece(part):
        def keep(sub, value):
            for xx in range(nx):
                for k in range(per):
                    piece[xx, sub * per + k, part] = value[
                        xx * rows_x : (xx + 1) * rows_x, k * quarter : (k + 1) * quarter
                    ]

        return keep

    end_a = HOP_Z * SUBS * ring_z.hops[0]
    end_b = HOP_Y * SUBS * ring_y.hops[0]
    events = []
    for sub in range(SUBS):
        events += ring(
            ring_z, (a0, a1), send_a, recv_a, sub, local_a, keep_a, z_at, z_peer, 0.0, HOP_Z
        )
        events += ring(
            ring_y, (b0, b1), send_b, recv_b, sub, local_b, keep_b, y_at, y_peer, 0.01, HOP_Y
        )
        events += ring(
            ring_y, (c0, c1), send_c, recv_c, sub, lambda yy, s: own_a[s, yy], keep_piece(0),
            y_at, y_peer, end_a + HOP_Z * sub + 0.1, HOP_SMALL / SUBS,
        )
        events += ring(
            ring_z, (d0, d1), send_d, recv_d, sub, lambda zz, s: own_b[s, zz], keep_piece(1),
            z_at, z_peer, end_b + HOP_Y * sub + 0.1, HOP_SMALL / SUBS,
        )
    for _, event in sorted(events, key=lambda pair: pair[0]):
        event()

    for xx, cc, dx, dc in others:
        if dc == 0:
            post(piece.at[xx], whole, send_e.at[dx, dc], recv_e.at[dx, dc], at(z, y, xx, cc))
        else:
            post(piece.at[xx, cc], got.at[dx, dc], send_e.at[dx, dc], recv_e.at[dx, dc], at(z, y, xx, cc))

    entries = dia_ref.shape[0]
    lanes = sum_y.shape[2]
    tile_id = dia_ref[:, 0:1]
    tile_row = tile_id >> 1
    tile_col = tile_id & 1
    key_lane = (dia_ref[:, 3:4] * 2 + tile_row) * (nc * nc) + dia_ref[:, 1:2] * nc + dia_ref[:, 2:3]
    is_lane = lax.broadcasted_iota(jnp.int32, (entries, lanes), 1) == key_lane
    pick = [is_lane & (tile_col == b) for b in range(2)]

    for dc in range(nc):
        if dc:
            for dx in range(nx):
                arrived(got.at[dx, dc], send_e.at[dx, dc], recv_e.at[dx, dc])
            value = got[0, dc]
            for dx in range(1, nx):
                value += got[dx, dc]
            total[lax.rem(cut - dc + nc, nc)] = value
        elif nx > 1:
            arrived(whole, send_e.at[1, 0], recv_e.at[1, 0])
            whole[...] += piece[x]
        else:
            whole[...] = piece[x]
    total[cut] = whole[cut]

    re = [total[t, 0] for t in range(nc)]
    im = [total[t, 1] for t in range(nc)]

    def down(value):
        return jnp.sum(value, axis=0, keepdims=True)

    rr, ii = {}, {}
    for s in range(nc):
        for t in range(s, nc):
            rr[s, t] = rr[t, s] = down(re[s] * re[t] + im[s] * im[t])
            if s == t:
                ii[s, t] = jnp.zeros_like(rr[s, t])
            else:
                ii[s, t] = down(im[s] * re[t] - re[s] * im[t])
                ii[t, s] = -ii[s, t]
    pairs = [(s, t) for s in range(nc) for t in range(nc)]
    key = z // (nz // (2 * PHASES))
    own_b_col = cut // 2
    lane_id = lax.broadcasted_iota(jnp.int32, (nc * nc, lanes), 1)
    row_id = lax.broadcasted_iota(jnp.int32, (nc * nc, lanes), 0)
    spot = lane_id == key * (nc * nc) + row_id
    tile_rows = lax.broadcasted_iota(jnp.int32, sum_y.shape[1:], 0)
    table = jnp.zeros(sum_y.shape[1:], jnp.float32)
    for part, values in enumerate((rr, ii)):
        column = jnp.sum(jnp.concatenate([values[p] for p in pairs], axis=0), axis=1, keepdims=True)
        lane_row = down(jnp.where(spot, column, 0.0))
        table = jnp.where(tile_rows == 2 * part + own_b_col, lane_row, table)

    def all_sum(table, slots, send_sems, recv_sems, me, count, targets):
        slots[me] = table
        for k, peer in enumerate(targets):
            post(slots.at[me], slots.at[me], send_sems.at[k], recv_sems.at[me], peer)
        for k in range(1, count):
            source = lax.rem(me + k, count)
            arrived(slots.at[source], send_sems.at[k - 1], recv_sems.at[source])
        value = slots[0]
        for k in range(1, count):
            value += slots[k]
        return value

    table = all_sum(table, sum_y, send_y, recv_y, y, ny, [at(z, y_at(k), x, cut) for k in range(1, ny)])

    for part in range(2):
        for k in range(nc):
            start = part * modes + k * quarter
            meson_ref[0, :, start : start + quarter] = whole[k, part]

    table = all_sum(
        table, sum_x, send_x, recv_x, x * nc + cut, nx * nc, [at(z, y, xx, cc) for xx, cc, _, _ in others]
    )
    table = all_sum(table, sum_z, send_z, recv_z, z, nz, [at(z_at(k), y, x, cut) for k in range(1, nz)])

    columns = []
    for part in range(2):
        value = jnp.where(pick[0], table[2 * part : 2 * part + 1], 0.0) + jnp.where(
            pick[1], table[2 * part + 1 : 2 * part + 2], 0.0
        )
        columns.append(jnp.sum(value, axis=1, keepdims=True) / TILE)
    value_ref[...] = jnp.concatenate(columns, axis=1)

    for copy in sends:
        copy.wait_send()


def per_device(vectors, momenta, diagrams):
    nz, ny, nx = RINGS
    modes, sites = vectors.shape[2:]
    rows = PHASES * modes
    rows_y = rows // (nz * ny)
    rows_z = rows_y * ny
    width = modes // SUBS
    quarter = modes // CUTS
    lanes = max(128, 2 * PHASES * CUTS * CUTS)
    depth = 6 * sites
    z_hops = Ring("z", nz, HOP_Z).hops
    y_hops = Ring("y", ny, HOP_Y).hops
    f32, bf16 = jnp.float32, jnp.bfloat16
    dma = pltpu.SemaphoreType.DMA

    def slots(hops, *shape):
        return [pltpu.VMEM((count + 1, SUBS, *shape), f32) for count in hops]

    def sems(hops):
        return [dma((2, hops[0], SUBS))] * 2

    scratch = [
        pltpu.VMEM((nz, ny, rows_y, depth), bf16),
        pltpu.VMEM((2 * modes, depth), bf16),
        *slots(z_hops, rows_z, width),
        *slots(y_hops, nz * rows_y, width),
        pltpu.VMEM((SUBS, ny, rows_y, width), f32),
        pltpu.VMEM((SUBS, nz, rows_y, width), f32),
        *slots(y_hops, rows_y, width),
        *slots(z_hops, rows_y, width),
        pltpu.VMEM((nx, CUTS, 2, rows_y // nx, quarter), f32),
        pltpu.VMEM((nx, CUTS, 2, rows_y // nx, quarter), f32),
        pltpu.VMEM((CUTS, 2, rows_y // nx, quarter), f32),
        pltpu.VMEM((CUTS, 2, rows_y // nx, quarter), f32),
        pltpu.VMEM((ny, 8, lanes), f32),
        pltpu.VMEM((nx * CUTS, 8, lanes), f32),
        pltpu.VMEM((nz, 8, lanes), f32),
        *sems(z_hops),
        *sems(y_hops),
        *sems(y_hops),
        *sems(z_hops),
        *[dma((nx, CUTS))] * 2,
        *[dma((ny,))] * 2,
        *[dma((nx * CUTS,))] * 2,
        *[dma((nz,))] * 2,
    ]
    vmem = pl.BlockSpec(memory_space=pltpu.VMEM)
    return pl.pallas_call(
        kernel,
        out_shape=(
            jax.ShapeDtypeStruct((1, rows_y // nx, 2 * modes), f32),
            jax.ShapeDtypeStruct((diagrams.shape[0], 2), f32),
        ),
        in_specs=[vmem, pl.BlockSpec(memory_space=pltpu.SMEM), vmem],
        out_specs=(vmem, vmem),
        scratch_shapes=scratch,
        compiler_params=pltpu.CompilerParams(
            collective_id=0, has_side_effects=True, vmem_limit_bytes=56 * 1024 * 1024
        ),
    )(vectors, momenta, diagrams)


def solution(mesh):
    return jax.shard_map(
        per_device,
        mesh=mesh,
        in_specs=(P("cuts", None, None, "space"), P(), P()),
        out_specs=(P("cuts", "space", None), P()),
        check_vma=False,
    )
```

time: 2310 us -> 104 us (0.05)
  the two profiles are of different devices: /device:TPU:2 before, /device:TPU:1 now
where the time goes in v1:
time: 104 us
  Pallas kernels  99.8 us (96%)
  local copies, waits for them, and re-layouts  3.41 us (3%)
    pallas_call x1, Pallas kernels, per_device(): pl.pallas_call(kernel, out_shape=(jax.ShapeDtypeStruct((1, rows_y // nx,...  99.8 us

profile of v1, /device:TPU:1, one launch (start us, length us, event | category | flops | bytes accessed | tf_op | source)
XLA Modules:
  0.0 103.9 jit_solution(7728425535693999884)
XLA Ops:
  0.6 1.4 %copy.5.dia_ref = s32[64,5]{1,0:T(8,128)} copy(s32[64,5]{0,1:T(8,128)} %param.5) | data formatting | bytes 2560 | tf_op args[2]
  2.0 99.8 %shard_map.50 = (f32[1,8,1024]{2,1,0:T(8,128)}, f32[64,2]{1,0:T(8,128)}) custom-call(f32[1,2,512,256]{3,2,1,0:T(8,128)} %vec_ref.1, s32[3,3]{1,0:T(4,128)} %mom_ref.1, s32[64,5]{1,0:T(8,128)} %copy.5.dia_ref), custom_call_target="tpu_custom_call" | custom-call | tf_op jit(solution)/shard_map/pallas_call | solution.py:421
  101.8 0.0 copy-start
  101.9 1.4 %copy.6 = f32[64,2]{0,1:T(2,128)} copy(f32[64,2]{1,0:T(8,128)} %get-tuple-element.3) | data formatting | bytes 1024 | tf_op jit(solution)/shard_map/pallas_call | solution.py:421
  103.3 0.0 copy-done
  103.3 0.6 copy.8
Async XLA Ops:
  101.8 1.4 %copy-start = (f32[1,8,1024]{2,1,0:T(8,128)S(1)}, f32[1,8,1024]{2,1,0:T(8,128)}, u32[]{:S(2)}) copy-start(f32[1,8,1024]{2,1,0:T(8,128)} %get-tuple-element.6) | copy-start | bytes 98308

commit v2 on v1

--- a/solution.py
+++ b/solution.py
@@ -14,7 +14,8 @@
 RINGS = (12, 8, 2)
 CUTS = 4
 SUBS = 2
-HOP_Z, HOP_Y, HOP_SMALL = 2.6, 3.9, 1.6
+HOP_Z, HOP_Y, ROUND = 2.6, 3.9, 4.0
+RELAY = 3
 
 full_turn = 2.0 * math.pi
 MESH = pl.DeviceIdType.MESH
@@ -32,18 +33,29 @@
     return high, low
 
 
-class Ring:
-    def __init__(self, name, extent, hop):
-        self.name, self.extent, self.hop = name, extent, hop
-        self.hops = (extent // 2, extent - 1 - extent // 2)
+def meet(extent):
+    return extent // 2, extent - 1 - extent // 2
+
+
+def far_first(extent):
+    return sorted(range(1, extent), key=lambda k: -min(k, extent - k))
+
+
+def relays(extent):
+    by_relay, straight = [], []
+    for side, count in enumerate(meet(extent)):
+        for distance in range(1, count + 1):
+            (by_relay if distance > RELAY else straight).append((side, distance))
+    return by_relay, straight
 
 
 def kernel(
-    vec_ref,
+    vec_hbm,
     mom_ref,
     dia_ref,
     meson_ref,
     value_ref,
+    vec_ref,
     left,
     right,
     a0,
@@ -52,10 +64,9 @@
     b1,
     own_a,
     own_b,
-    c0,
-    c1,
-    d0,
-    d1,
+    in_c,
+    relay_d,
+    in_d,
     piece,
     got,
     whole,
@@ -63,6 +74,7 @@
     sum_y,
     sum_x,
     sum_z,
+    load_sem,
     send_a,
     recv_a,
     send_b,
@@ -70,9 +82,12 @@
     send_c,
     recv_c,
     send_d,
+    recv_relay,
     recv_d,
     send_e,
     recv_e,
+    send_whole,
+    recv_whole,
     send_y,
     recv_y,
     send_x,
@@ -82,7 +97,7 @@
 ):
     nz, ny, nx = RINGS
     nc = CUTS
-    modes, sites = vec_ref.shape[2:]
+    modes, sites = vec_ref.shape[1:]
     width = modes // SUBS
     rows_y = left.shape[2]
     rows_z = ny * rows_y
@@ -104,12 +119,15 @@
     def y_at(step):
         return lax.rem(y + step + 2 * ny, ny)
 
+    load = pltpu.make_async_copy(vec_hbm.at[0], vec_ref, load_sem)
+    load.start()
+
     peers = [at(z_at(k), y, x, cut) for k in range(1, nz)]
     peers += [at(z, y_at(k), x, cut) for k in range(1, ny)]
     others = [
         (lax.rem(x + dx, nx), lax.rem(cut + dc, nc), dx, dc)
-        for dx in range(nx)
-        for dc in range(nc)
+        for dx in reversed(range(nx))
+        for dc in (2, 1, 3, 0)
         if dx or dc
     ]
     peers += [at(z, y, xx, cc) for xx, cc, _, _ in others]
@@ -117,8 +135,9 @@
     for peer in peers:
         pl.semaphore_signal(barrier, inc=1, device_id=peer, device_id_type=MESH)
 
-    real_vec = vec_ref[0, 0]
-    imag_vec = vec_ref[0, 1]
+    load.wait()
+    real_vec = vec_ref[0]
+    imag_vec = vec_ref[1]
     depth = 2 * sites
     rh, rl = halves(real_vec)
     ih, il = halves(imag_vec)
@@ -159,7 +178,6 @@
                 left[zz, yy, :, depth + cols : depth + cols + sites] = low[rows]
                 left[zz, yy, :, 2 * depth + cols : 2 * depth + cols + sites] = high[rows]
 
-    pl.semaphore_wait(barrier, len(peers))
     sends = []
 
     def post(source, target, send_sem, recv_sem, peer):
@@ -193,22 +211,17 @@
         start = modes + sub * width
         return contract(rows, right[start : start + width, :])
 
-    def ring(ring_of, slots, send_sems, recv_sems, sub, local, finish, step_at, peer_of, start, tick):
-        hops = ring_of.hops
-
+    def ring(hops, slots, send_sems, recv_sems, sub, local, finish, step_at, peer_of, tick):
         def hop(direction, step):
             way = sign if direction == 0 else -sign
-            buffer = slots[direction]
-            here = buffer.at[step, sub]
+            here = slots[direction].at[step, sub]
             if step:
                 mine = local(step_at(way * (hops[direction] - step)), sub)
                 arrived(here, send_sems.at[direction, step - 1, sub], recv_sems.at[direction, step - 1, sub])
                 here[...] += mine
-            else:
-                here[...] = local(step_at(way * hops[direction]), sub)
             post(
                 here,
-                buffer.at[step + 1, sub],
+                slots[direction].at[step + 1, sub],
                 send_sems.at[direction, step, sub],
                 recv_sems.at[direction, step, sub],
                 peer_of(way),
@@ -224,10 +237,18 @@
                     value += here[...]
             finish(sub, value)
 
+        made = []
         for direction in (0, 1):
             for step in range(hops[direction]):
-                yield start + tick * (step * SUBS + sub), functools.partial(hop, direction, step)
-        yield start + tick * (hops[0] * SUBS + sub), last
+                made.append((tick * (step * SUBS + sub), functools.partial(hop, direction, step)))
+        made.append((tick * (hops[0] * SUBS + sub), last))
+        return made
+
+    def first_chunks(hops, slots, sub, local, step_at):
+        for direction in (0, 1):
+            if hops[direction]:
+                way = sign if direction == 0 else -sign
+                slots[direction][0, sub] = local(step_at(way * hops[direction]), sub)
 
     def z_peer(way):
         return at(z_at(way), y, x, cut)
@@ -235,77 +256,128 @@
     def y_peer(way):
         return at(z, y_at(way), x, cut)
 
-    ring_z = Ring("z", nz, HOP_Z)
-    ring_y = Ring("y", ny, HOP_Y)
-
-    def keep_a(sub, value):
+    def way_of(side):
+        return sign if side == 0 else -sign
+
+    hops_z, hops_y = meet(nz), meet(ny)
+    per = width // quarter
+
+    def keep(part, sub, value):
+        for xx in range(nx):
+            for k in range(per):
+                piece[xx, sub * per + k, part] = value[
+                    xx * rows_x : (xx + 1) * rows_x, k * quarter : (k + 1) * quarter
+                ]
+
+    def spread_a(sub, value):
         own_a[sub] = value.reshape(ny, rows_y, width)
-
-    def keep_b(sub, value):
+        for k in far_first(ny):
+            post(
+                own_a.at[sub, y_at(k)], in_c.at[sub, k - 1], send_c.at[sub, k - 1], recv_c.at[sub, k - 1], y_peer(k)
+            )
+
+    def gather_a(sub):
+        value = own_a[sub, y]
+        for k in far_first(ny)[::-1]:
+            arrived(in_c.at[sub, k - 1], send_c.at[sub, k - 1], recv_c.at[sub, k - 1])
+            value += in_c[sub, k - 1]
+        keep(0, sub, value)
+
+    by_relay, straight = relays(nz)
+
+    def spread_b(sub, value):
         own_b[sub] = value.reshape(nz, rows_y, width)
-
-    per = width // quarter
-
-    def keep_piece(part):
-        def keep(sub, value):
-            for xx in range(nx):
-                for k in range(per):
-                    piece[xx, sub * per + k, part] = value[
-                        xx * rows_x : (xx + 1) * rows_x, k * quarter : (k + 1) * quarter
-                    ]
-
-        return keep
-
-    end_a = HOP_Z * SUBS * ring_z.hops[0]
-    end_b = HOP_Y * SUBS * ring_y.hops[0]
+        for k, (side, distance) in sorted(enumerate(by_relay), key=lambda item: -item[1][1]):
+            way = way_of(side)
+            post(
+                own_b.at[sub, z_at(-way * distance)],
+                relay_d.at[sub, k],
+                send_d.at[sub, k],
+                recv_relay.at[sub, k],
+                z_peer(-way * (distance - RELAY)),
+            )
+        for k, (side, distance) in sorted(enumerate(straight), key=lambda item: -item[1][1]):
+            if not has_relay(side, distance):
+                send_straight(sub, k, side, distance)
+
+    def has_relay(side, distance):
+        return distance == RELAY and any(other == side for other, _ in by_relay)
+
+    def send_straight(sub, k, side, distance):
+        way = way_of(side)
+        post(
+            own_b.at[sub, z_at(-way * distance)],
+            in_d.at[sub, k],
+            send_d.at[sub, len(by_relay) + k],
+            recv_d.at[sub, k],
+            z_peer(-way * distance),
+        )
+
+    def relay_b(sub):
+        for k, (side, distance) in enumerate(straight):
+            if has_relay(side, distance):
+                spot = z_at(-way_of(side) * distance)
+                value = own_b[sub, spot]
+                for j, (other, _) in enumerate(by_relay):
+                    if other == side:
+                        arrived(relay_d.at[sub, j], send_d.at[sub, j], recv_relay.at[sub, j])
+                        value += relay_d[sub, j]
+                own_b[sub, spot] = value
+                send_straight(sub, k, side, distance)
+
+    def gather_b(sub):
+        value = own_b[sub, z]
+        for k, (side, distance) in enumerate(straight):
+            arrived(in_d.at[sub, k], send_d.at[sub, len(by_relay) + k], recv_d.at[sub, k])
+            value += in_d[sub, k]
+        keep(1, sub, value)
+
     events = []
     for sub in range(SUBS):
-        events += ring(
-            ring_z, (a0, a1), send_a, recv_a, sub, local_a, keep_a, z_at, z_peer, 0.0, HOP_Z
-        )
-        events += ring(
-            ring_y, (b0, b1), send_b, recv_b, sub, local_b, keep_b, y_at, y_peer, 0.01, HOP_Y
-        )
-        events += ring(
-            ring_y, (c0, c1), send_c, recv_c, sub, lambda yy, s: own_a[s, yy], keep_piece(0),
-            y_at, y_peer, end_a + HOP_Z * sub + 0.1, HOP_SMALL / SUBS,
-        )
-        events += ring(
-            ring_z, (d0, d1), send_d, recv_d, sub, lambda zz, s: own_b[s, zz], keep_piece(1),
-            z_at, z_peer, end_b + HOP_Y * sub + 0.1, HOP_SMALL / SUBS,
-        )
+        first_chunks(hops_z, (a0, a1), sub, local_a, z_at)
+        first_chunks(hops_y, (b0, b1), sub, local_b, y_at)
+        events += ring(hops_z, (a0, a1), send_a, recv_a, sub, local_a, spread_a, z_at, z_peer, HOP_Z)
+        end = events[-1][0]
+        events.append((end + 1.5 * ROUND, functools.partial(gather_a, sub)))
+        events += ring(hops_y, (b0, b1), send_b, recv_b, sub, local_b, spread_b, y_at, y_peer, HOP_Y)
+        end = events[-1][0]
+        events.append((end + ROUND, functools.partial(relay_b, sub)))
+        events.append((end + 2 * ROUND, functools.partial(gather_b, sub)))
+
+    pl.semaphore_wait(barrier, len(peers))
     for _, event in sorted(events, key=lambda pair: pair[0]):
         event()
 
     for xx, cc, dx, dc in others:
-        if dc == 0:
-            post(piece.at[xx], whole, send_e.at[dx, dc], recv_e.at[dx, dc], at(z, y, xx, cc))
-        else:
-            post(piece.at[xx, cc], got.at[dx, dc], send_e.at[dx, dc], recv_e.at[dx, dc], at(z, y, xx, cc))
-
-    entries = dia_ref.shape[0]
+        post(piece.at[xx, cc], got.at[dx, dc], send_e.at[dx, dc], recv_e.at[dx, dc], at(z, y, xx, cc))
+    for dx in range(1, nx):
+        xx = lax.rem(x + dx, nx)
+        post(piece.at[xx], whole.at[dx], send_whole.at[dx], recv_whole.at[dx], at(z, y, xx, cut))
+
+    entries = dia_ref.shape[1]
     lanes = sum_y.shape[2]
-    tile_id = dia_ref[:, 0:1]
-    tile_row = tile_id >> 1
-    tile_col = tile_id & 1
-    key_lane = (dia_ref[:, 3:4] * 2 + tile_row) * (nc * nc) + dia_ref[:, 1:2] * nc + dia_ref[:, 2:3]
-    is_lane = lax.broadcasted_iota(jnp.int32, (entries, lanes), 1) == key_lane
-    pick = [is_lane & (tile_col == b) for b in range(2)]
+    tile_id = dia_ref[0:1, :]
+    code = (
+        (dia_ref[3:4, :] * 2 + (tile_id >> 1)) * (nc * nc)
+        + dia_ref[1:2, :] * nc
+        + dia_ref[2:3, :]
+        + (tile_id & 1) * lanes
+    ).astype(jnp.float32)
+    eye = lax.broadcasted_iota(jnp.int32, (entries, entries), 0) == lax.broadcasted_iota(
+        jnp.int32, (entries, entries), 1
+    )
+    code = jnp.sum(jnp.where(eye, code, 0.0), axis=1, keepdims=True)
+    lane_code = lax.broadcasted_iota(jnp.int32, (entries, lanes), 1).astype(jnp.float32)
+    pick = [lane_code + float(b * lanes) == code for b in range(2)]
 
     for dc in range(nc):
-        if dc:
-            for dx in range(nx):
+        for dx in range(nx):
+            if dx or dc:
                 arrived(got.at[dx, dc], send_e.at[dx, dc], recv_e.at[dx, dc])
-            value = got[0, dc]
-            for dx in range(1, nx):
-                value += got[dx, dc]
-            total[lax.rem(cut - dc + nc, nc)] = value
-        elif nx > 1:
-            arrived(whole, send_e.at[1, 0], recv_e.at[1, 0])
-            whole[...] += piece[x]
-        else:
-            whole[...] = piece[x]
-    total[cut] = whole[cut]
+        value = got[0, dc] if dc else piece[x, cut]
+        for dx in range(1, nx):
+            value += got[dx, dc]
+        total[lax.rem(cut - dc + nc, nc)] = value
 
     re = [total[t, 0] for t in range(nc)]
     im = [total[t, 1] for t in range(nc)]
@@ -347,25 +419,28 @@
             value += slots[k]
         return value
 
-    table = all_sum(table, sum_y, send_y, recv_y, y, ny, [at(z, y_at(k), x, cut) for k in range(1, ny)])
-
+    table = all_sum(table, sum_y, send_y, recv_y, y, ny, [at(z, y_at(k), x, cut) for k in far_first(ny)])
+
+    rows_own = piece[x]
+    for dx in range(1, nx):
+        arrived(whole.at[dx], send_whole.at[dx], recv_whole.at[dx])
+        rows_own += whole[dx]
     for part in range(2):
         for k in range(nc):
             start = part * modes + k * quarter
-            meson_ref[0, :, start : start + quarter] = whole[k, part]
+            meson_ref[0, :, start : start + quarter] = rows_own[k, part]
 
     table = all_sum(
         table, sum_x, send_x, recv_x, x * nc + cut, nx * nc, [at(z, y, xx, cc) for xx, cc, _, _ in others]
     )
-    table = all_sum(table, sum_z, send_z, recv_z, z, nz, [at(z_at(k), y, x, cut) for k in range(1, nz)])
-
-    columns = []
+    table = all_sum(table, sum_z, send_z, recv_z, z, nz, [at(z_at(k), y, x, cut) for k in far_first(nz)])
+
     for part in range(2):
         value = jnp.where(pick[0], table[2 * part : 2 * part + 1], 0.0) + jnp.where(
             pick[1], table[2 * part + 1 : 2 * part + 2], 0.0
         )
-        columns.append(jnp.sum(value, axis=1, keepdims=True) / TILE)
-    value_ref[...] = jnp.concatenate(columns, axis=1)
+        column = jnp.sum(value, axis=1, keepdims=True)
+        value_ref[part : part + 1, :] = down(jnp.where(eye, column, 0.0)) / TILE
 
     for copy in sends:
         copy.wait_send()
@@ -381,8 +456,8 @@
     quarter = modes // CUTS
     lanes = max(128, 2 * PHASES * CUTS * CUTS)
     depth = 6 * sites
-    z_hops = Ring("z", nz, HOP_Z).hops
-    y_hops = Ring("y", ny, HOP_Y).hops
+    z_hops, y_hops = meet(nz), meet(ny)
+    by_relay, straight = relays(nz)
     f32, bf16 = jnp.float32, jnp.bfloat16
     dma = pltpu.SemaphoreType.DMA
 
@@ -393,44 +468,51 @@
         return [dma((2, hops[0], SUBS))] * 2
 
     scratch = [
+        pltpu.VMEM(vectors.shape[1:], f32),
         pltpu.VMEM((nz, ny, rows_y, depth), bf16),
         pltpu.VMEM((2 * modes, depth), bf16),
         *slots(z_hops, rows_z, width),
         *slots(y_hops, nz * rows_y, width),
         pltpu.VMEM((SUBS, ny, rows_y, width), f32),
         pltpu.VMEM((SUBS, nz, rows_y, width), f32),
-        *slots(y_hops, rows_y, width),
-        *slots(z_hops, rows_y, width),
+        pltpu.VMEM((SUBS, ny - 1, rows_y, width), f32),
+        pltpu.VMEM((SUBS, max(1, len(by_relay)), rows_y, width), f32),
+        pltpu.VMEM((SUBS, len(straight), rows_y, width), f32),
         pltpu.VMEM((nx, CUTS, 2, rows_y // nx, quarter), f32),
         pltpu.VMEM((nx, CUTS, 2, rows_y // nx, quarter), f32),
-        pltpu.VMEM((CUTS, 2, rows_y // nx, quarter), f32),
+        pltpu.VMEM((nx, CUTS, 2, rows_y // nx, quarter), f32),
         pltpu.VMEM((CUTS, 2, rows_y // nx, quarter), f32),
         pltpu.VMEM((ny, 8, lanes), f32),
         pltpu.VMEM((nx * CUTS, 8, lanes), f32),
         pltpu.VMEM((nz, 8, lanes), f32),
+        dma,
         *sems(z_hops),
         *sems(y_hops),
-        *sems(y_hops),
-        *sems(z_hops),
+        *[dma((SUBS, ny - 1))] * 2,
+        dma((SUBS, nz - 1)),
+        dma((SUBS, max(1, len(by_relay)))),
+        dma((SUBS, len(straight))),
         *[dma((nx, CUTS))] * 2,
+        *[dma((nx,))] * 2,
         *[dma((ny,))] * 2,
         *[dma((nx * CUTS,))] * 2,
         *[dma((nz,))] * 2,
     ]
     vmem = pl.BlockSpec(memory_space=pltpu.VMEM)
-    return pl.pallas_call(
+    meson, values = pl.pallas_call(
         kernel,
         out_shape=(
             jax.ShapeDtypeStruct((1, rows_y // nx, 2 * modes), f32),
-            jax.ShapeDtypeStruct((diagrams.shape[0], 2), f32),
+            jax.ShapeDtypeStruct((2, diagrams.shape[0]), f32),
         ),
-        in_specs=[vmem, pl.BlockSpec(memory_space=pltpu.SMEM), vmem],
+        in_specs=[pl.BlockSpec(memory_space=pl.ANY), pl.BlockSpec(memory_space=pltpu.SMEM), vmem],
         out_specs=(vmem, vmem),
         scratch_shapes=scratch,
         compiler_params=pltpu.CompilerParams(
             collective_id=0, has_side_effects=True, vmem_limit_bytes=56 * 1024 * 1024
         ),
-    )(vectors, momenta, diagrams)
+    )(vectors, momenta, diagrams.T)
+    return meson, values.T
 
 
 def solution(mesh):

time: 104 us -> 91.2 us (0.88)
  Pallas kernels: 99.8 us -> 88.4 us
  local copies, waits for them, and re-layouts: 3.41 us -> 1.94 us
    pallas_call x1, Pallas kernels: 99.8 us -> 88.4 us  [per_device(): pl.pallas_call(kernel, out_shape=(jax.ShapeDtypeStruct((1, rows_y // nx,...]
    pallas_call x1 -> x0, local copies, waits for them, and re-layouts: 1.4 us -> none  [per_device(): pl.pallas_call(kernel, out_shape=(jax.ShapeDtypeStruct((1, rows_y // nx,...]
where the time goes in v2:
time: 91.2 us; the launch traced here: 91 us
  Pallas kernels  88.4 us (97%)
  local copies, waits for them, and re-layouts  1.94 us (2%)
    pallas_call x1, Pallas kernels, per_device(): pl.pallas_call(kernel, out_shape=(jax.ShapeDtypeStruct((1, rows_y // nx,...  88.4 us
    unnamed x4, local copies, waits for them, and re-layouts  1.94 us

profile of v2, /device:TPU:1, one launch (start us, length us, event | category | flops | bytes accessed | tf_op | source)
XLA Modules:
  0.0 91.0 jit_solution(2464821531218335014)
XLA Ops:
  0.6 88.4 %shard_map.50 = (f32[1,8,1024]{2,1,0:T(8,128)}, f32[2,64]{1,0:T(2,128)}) custom-call(f32[1,2,512,256]{3,2,1,0:T(8,128)} %vec_hbm.1, s32[3,3]{1,0:T(4,128)} %mom_ref.1, s32[5,64]{1,0:T(8,128)} %bitcast.2), custom_call_target="tpu_custom_call" | custom-call | tf_op jit(solution)/shard_map/pallas_call | solution.py:502
  89.0 0.0 copy-start
  89.0 1.4 %copy.7 = f32[1,8,1024]{2,1,0:T(8,128)} copy(f32[1,8,1024]{2,1,0:T(8,128)} %get-tuple-element.8) | data formatting | bytes 65536
  90.4 0.0 copy-done
  90.4 0.6 copy.8
Async XLA Ops:
  89.0 1.4 %copy-start = (f32[2,64]{1,0:T(2,128)S(1)}, f32[2,64]{1,0:T(2,128)}, u32[]{:S(2)}) copy-start(f32[2,64]{1,0:T(2,128)} %get-tuple-element.5) | copy-start | bytes 1540

commit v3 on v2

--- a/solution.py
+++ b/solution.py
@@ -122,8 +122,8 @@
     load = pltpu.make_async_copy(vec_hbm.at[0], vec_ref, load_sem)
     load.start()
 
-    peers = [at(z_at(k), y, x, cut) for k in range(1, nz)]
-    peers += [at(z, y_at(k), x, cut) for k in range(1, ny)]
+    peers = [at(z_at(k), y, x, cut) for k in sorted({1, nz - 1})]
+    peers += [at(z, y_at(k), x, cut) for k in sorted({1, ny - 1})]
     others = [
         (lax.rem(x + dx, nx), lax.rem(cut + dc, nc), dx, dc)
         for dx in reversed(range(nx))
@@ -202,34 +202,45 @@
             device_id_type=MESH,
         ).wait_recv()
 
-    def local_a(zz, sub):
-        rows = left[zz].reshape(rows_z, left.shape[3])
-        return contract(rows, right[sub * width : (sub + 1) * width, :])
-
-    def local_b(yy, sub):
-        rows = left[:, yy].reshape(nz * rows_y, left.shape[3])
+    def local_a(spots, sub):
+        rows = [left[zz].reshape(rows_z, left.shape[3]) for zz in spots]
+        made = contract(jnp.concatenate(rows, axis=0), right[sub * width : (sub + 1) * width, :])
+        return [made[k * rows_z : (k + 1) * rows_z] for k in range(len(spots))]
+
+    def local_b(spots, sub):
+        high = nz * rows_y
+        rows = [left[:, yy].reshape(high, left.shape[3]) for yy in spots]
         start = modes + sub * width
-        return contract(rows, right[start : start + width, :])
-
-    def ring(hops, slots, send_sems, recv_sems, sub, local, finish, step_at, peer_of, tick):
-        def hop(direction, step):
-            way = sign if direction == 0 else -sign
-            here = slots[direction].at[step, sub]
-            if step:
-                mine = local(step_at(way * (hops[direction] - step)), sub)
-                arrived(here, send_sems.at[direction, step - 1, sub], recv_sems.at[direction, step - 1, sub])
-                here[...] += mine
-            post(
-                here,
-                slots[direction].at[step + 1, sub],
-                send_sems.at[direction, step, sub],
-                recv_sems.at[direction, step, sub],
-                peer_of(way),
-            )
+        made = contract(jnp.concatenate(rows, axis=0), right[start : start + width, :])
+        return [made[k * high : (k + 1) * high] for k in range(len(spots))]
+
+    def ring(hops, slots, own, send_sems, recv_sems, sub, local, finish, step_at, peer_of, tick):
+        def hop(step):
+            ways = [(0, sign)] + ([(1, -sign)] if step < hops[1] else [])
+            spots = [step_at(way * (hops[direction] - step)) for direction, way in ways]
+            if step == hops[1]:
+                spots.append(step_at(0))
+            made = local(spots, sub)
+            for (direction, way), mine in zip(ways, made):
+                here = slots[direction].at[step, sub]
+                if step:
+                    arrived(here, send_sems.at[direction, step - 1, sub], recv_sems.at[direction, step - 1, sub])
+                    here[...] += mine
+                else:
+                    here[...] = mine
+                post(
+                    here,
+                    slots[direction].at[step + 1, sub],
+                    send_sems.at[direction, step, sub],
+                    recv_sems.at[direction, step, sub],
+                    peer_of(way),
+                )
+            if step == hops[1]:
+                own[sub] = made[1].reshape(own.shape[1:])
 
         def last():
-            value = local(step_at(0), sub)
-            for direction in (0, 1):
+            value = own[sub].reshape(slots[0].shape[2:]) if hops[0] > hops[1] else local([step_at(0)], sub)[0]
+            for direction in (1, 0):
                 count = hops[direction]
                 if count:
                     here = slots[direction].at[count, sub]
@@ -237,18 +248,9 @@
                     value += here[...]
             finish(sub, value)
 
-        made = []
-        for direction in (0, 1):
-            for step in range(hops[direction]):
-                made.append((tick * (step * SUBS + sub), functools.partial(hop, direction, step)))
+        made = [(tick * (step * SUBS + sub), functools.partial(hop, step)) for step in range(hops[0])]
         made.append((tick * (hops[0] * SUBS + sub), last))
         return made
-
-    def first_chunks(hops, slots, sub, local, step_at):
-        for direction in (0, 1):
-            if hops[direction]:
-                way = sign if direction == 0 else -sign
-                slots[direction][0, sub] = local(step_at(way * hops[direction]), sub)
 
     def z_peer(way):
         return at(z_at(way), y, x, cut)
@@ -334,15 +336,13 @@
 
     events = []
     for sub in range(SUBS):
-        first_chunks(hops_z, (a0, a1), sub, local_a, z_at)
-        first_chunks(hops_y, (b0, b1), sub, local_b, y_at)
-        events += ring(hops_z, (a0, a1), send_a, recv_a, sub, local_a, spread_a, z_at, z_peer, HOP_Z)
-        end = events[-1][0]
-        events.append((end + 1.5 * ROUND, functools.partial(gather_a, sub)))
-        events += ring(hops_y, (b0, b1), send_b, recv_b, sub, local_b, spread_b, y_at, y_peer, HOP_Y)
+        events += ring(hops_y, (b0, b1), own_b, send_b, recv_b, sub, local_b, spread_b, y_at, y_peer, HOP_Y)
         end = events[-1][0]
         events.append((end + ROUND, functools.partial(relay_b, sub)))
         events.append((end + 2 * ROUND, functools.partial(gather_b, sub)))
+        events += ring(hops_z, (a0, a1), own_a, send_a, recv_a, sub, local_a, spread_a, z_at, z_peer, HOP_Z)
+        events[-1] = (end + 0.1, events[-1][1])
+        events.append((end + 1.5 * ROUND, functools.partial(gather_a, sub)))
 
     pl.semaphore_wait(barrier, len(peers))
     for _, event in sorted(events, key=lambda pair: pair[0]):

time: 91.2 us -> 87.2 us (0.956)
  Pallas kernels: 88.4 us -> 84.4 us
    pallas_call x1, Pallas kernels: 88.4 us -> 84.4 us  [per_device(): pl.pallas_call(kernel, out_shape=(jax.ShapeDtypeStruct((1, rows_y // nx,...]
where the time goes in v3:
time: 87.2 us; the launch traced here: 86.9 us
  Pallas kernels  84.4 us (97%)
  local copies, waits for them, and re-layouts  1.94 us (2%)
    pallas_call x1, Pallas kernels, per_device(): pl.pallas_call(kernel, out_shape=(jax.ShapeDtypeStruct((1, rows_y // nx,...  84.4 us
    unnamed x4, local copies, waits for them, and re-layouts  1.94 us

profile of v3, /device:TPU:1, one launch (start us, length us, event | category | flops | bytes accessed | tf_op | source)
XLA Modules:
  0.0 86.9 jit_solution(10676525353848464021)
XLA Ops:
  0.6 84.4 %shard_map.50 = (f32[1,8,1024]{2,1,0:T(8,128)}, f32[2,64]{1,0:T(2,128)}) custom-call(f32[1,2,512,256]{3,2,1,0:T(8,128)} %vec_hbm.1, s32[3,3]{1,0:T(4,128)} %mom_ref.1, s32[5,64]{1,0:T(8,128)} %bitcast.2), custom_call_target="tpu_custom_call" | custom-call | tf_op jit(solution)/shard_map/pallas_call | solution.py:502
  85.0 0.0 copy-start
  85.0 1.4 %copy.7 = f32[1,8,1024]{2,1,0:T(8,128)} copy(f32[1,8,1024]{2,1,0:T(8,128)} %get-tuple-element.8) | data formatting | bytes 65536
  86.4 0.0 copy-done
  86.4 0.6 copy.8
Async XLA Ops:
  85.0 1.4 %copy-start = (f32[2,64]{1,0:T(2,128)S(1)}, f32[2,64]{1,0:T(2,128)}, u32[]{:S(2)}) copy-start(f32[2,64]{1,0:T(2,128)} %get-tuple-element.5) | copy-start | bytes 1540

commit v4 on v3

--- a/solution.py
+++ b/solution.py
@@ -502,8 +502,8 @@
     meson, values = pl.pallas_call(
         kernel,
         out_shape=(
-            jax.ShapeDtypeStruct((1, rows_y // nx, 2 * modes), f32),
-            jax.ShapeDtypeStruct((2, diagrams.shape[0]), f32),
+            pltpu.VMEM((1, rows_y // nx, 2 * modes), f32),
+            pltpu.VMEM((2, diagrams.shape[0]), f32),
         ),
         in_specs=[pl.BlockSpec(memory_space=pl.ANY), pl.BlockSpec(memory_space=pltpu.SMEM), vmem],
         out_specs=(vmem, vmem),

time: 87.2 us -> 85.8 us (0.984)
    unnamed x4 -> x2, local copies, waits for them, and re-layouts: 1.94 us -> 1.18 us
where the time goes in v4:
time: 85.8 us; the launch traced here: 85.6 us
  Pallas kernels  83.8 us (98%)
  local copies, waits for them, and re-layouts  1.18 us (1%)
    pallas_call x1, Pallas kernels, per_device(): pl.pallas_call(kernel, out_shape=(pltpu.VMEM((1, rows_y // nx, 2 * modes)...  83.8 us

profile of v4, /device:TPU:1, one launch (start us, length us, event | category | flops | bytes accessed | tf_op | source)
XLA Modules:
  0.0 85.6 jit_solution(5884017895619088893)
XLA Ops:
  0.6 83.8 %shard_map.50 = (f32[1,8,1024]{2,1,0:T(8,128)S(1)}, f32[2,64]{1,0:T(2,128)S(1)}) custom-call(f32[1,2,512,256]{3,2,1,0:T(8,128)} %vec_hbm.1, s32[3,3]{1,0:T(4,128)} %mom_ref.1, s32[5,64]{1,0:T(8,128)} %bitcast.3), custom_call_target="tpu_custom_call" | custom-call | tf_op jit(solution)/shard_map/pallas_call | solution.py:502
  84.4 0.6 copy.7
  85.0 0.6 copy.8

commit v5 on v4

--- a/solution.py
+++ b/solution.py
@@ -214,7 +214,7 @@
         made = contract(jnp.concatenate(rows, axis=0), right[start : start + width, :])
         return [made[k * high : (k + 1) * high] for k in range(len(spots))]
 
-    def ring(hops, slots, own, send_sems, recv_sems, sub, local, finish, step_at, peer_of, tick):
+    def ring(hops, slots, own, send_sems, recv_sems, sub, local, finish, step_at, peer_of, start, tick):
         def hop(step):
             ways = [(0, sign)] + ([(1, -sign)] if step < hops[1] else [])
             spots = [step_at(way * (hops[direction] - step)) for direction, way in ways]
@@ -248,8 +248,8 @@
                     value += here[...]
             finish(sub, value)
 
-        made = [(tick * (step * SUBS + sub), functools.partial(hop, step)) for step in range(hops[0])]
-        made.append((tick * (hops[0] * SUBS + sub), last))
+        made = [(start + tick * (step * SUBS + sub), functools.partial(hop, step)) for step in range(hops[0])]
+        made.append((start + tick * (hops[0] * SUBS + sub), last))
         return made
 
     def z_peer(way):
@@ -334,22 +334,42 @@
             value += in_d[sub, k]
         keep(1, sub, value)
 
+    quarters = []
+
+    def exchange(sub):
+        for quarter_id in range(sub * per, (sub + 1) * per):
+            for dx in reversed(range(nx)):
+                xx = lax.rem(x + dx, nx)
+                copy = pltpu.make_async_remote_copy(
+                    src_ref=piece.at[xx, quarter_id],
+                    dst_ref=got.at[dx, cut],
+                    send_sem=send_e.at[dx, quarter_id],
+                    recv_sem=recv_e.at[dx, cut],
+                    device_id=at(z, y, xx, quarter_id),
+                    device_id_type=MESH,
+                )
+                if dx:
+                    copy.start()
+                    sends.append(copy)
+                else:
+                    pl.when(cut != quarter_id)(copy.start)
+                    quarters.append((quarter_id, copy))
+
     events = []
     for sub in range(SUBS):
-        events += ring(hops_y, (b0, b1), own_b, send_b, recv_b, sub, local_b, spread_b, y_at, y_peer, HOP_Y)
+        events += ring(hops_y, (b0, b1), own_b, send_b, recv_b, sub, local_b, spread_b, y_at, y_peer, 0.01, HOP_Y)
         end = events[-1][0]
         events.append((end + ROUND, functools.partial(relay_b, sub)))
         events.append((end + 2 * ROUND, functools.partial(gather_b, sub)))
-        events += ring(hops_z, (a0, a1), own_a, send_a, recv_a, sub, local_a, spread_a, z_at, z_peer, HOP_Z)
+        events += ring(hops_z, (a0, a1), own_a, send_a, recv_a, sub, local_a, spread_a, z_at, z_peer, 0.0, HOP_Z)
         events[-1] = (end + 0.1, events[-1][1])
         events.append((end + 1.5 * ROUND, functools.partial(gather_a, sub)))
+        events.append((end + 2 * ROUND + 0.1, functools.partial(exchange, sub)))
 
     pl.semaphore_wait(barrier, len(peers))
     for _, event in sorted(events, key=lambda pair: pair[0]):
         event()
 
-    for xx, cc, dx, dc in others:
-        post(piece.at[xx, cc], got.at[dx, dc], send_e.at[dx, dc], recv_e.at[dx, dc], at(z, y, xx, cc))
     for dx in range(1, nx):
         xx = lax.rem(x + dx, nx)
         post(piece.at[xx], whole.at[dx], send_whole.at[dx], recv_whole.at[dx], at(z, y, xx, cut))
@@ -370,14 +390,19 @@
     lane_code = lax.broadcasted_iota(jnp.int32, (entries, lanes), 1).astype(jnp.float32)
     pick = [lane_code + float(b * lanes) == code for b in range(2)]
 
-    for dc in range(nc):
-        for dx in range(nx):
-            if dx or dc:
-                arrived(got.at[dx, dc], send_e.at[dx, dc], recv_e.at[dx, dc])
-        value = got[0, dc] if dc else piece[x, cut]
+    got[0, cut] = piece[x, cut]
+    for t in range(nc):
+        for dx in reversed(range(nx)):
+            take = functools.partial(arrived, got.at[dx, t], send_e.at[dx, t], recv_e.at[dx, t])
+            if dx:
+                take()
+            else:
+                pl.when(cut != t)(take)
+    for t in range(nc):
+        value = got[0, t]
         for dx in range(1, nx):
-            value += got[dx, dc]
-        total[lax.rem(cut - dc + nc, nc)] = value
+            value += got[dx, t]
+        total[t] = value
 
     re = [total[t, 0] for t in range(nc)]
     im = [total[t, 1] for t in range(nc)]
@@ -407,10 +432,15 @@
         lane_row = down(jnp.where(spot, column, 0.0))
         table = jnp.where(tile_rows == 2 * part + own_b_col, lane_row, table)
 
-    def all_sum(table, slots, send_sems, recv_sems, me, count, targets):
+    def all_sum(table, slots, send_sems, recv_sems, me, count, targets, meanwhile):
+        earlier = list(sends)
+        sends.clear()
         slots[me] = table
         for k, peer in enumerate(targets):
             post(slots.at[me], slots.at[me], send_sems.at[k], recv_sems.at[me], peer)
+        for copy in earlier:
+            copy.wait_send()
+        meanwhile()
         for k in range(1, count):
             source = lax.rem(me + k, count)
             arrived(slots.at[source], send_sems.at[k - 1], recv_sems.at[source])
@@ -419,21 +449,21 @@
             value += slots[k]
         return value
 
-    table = all_sum(table, sum_y, send_y, recv_y, y, ny, [at(z, y_at(k), x, cut) for k in far_first(ny)])
-
-    rows_own = piece[x]
-    for dx in range(1, nx):
-        arrived(whole.at[dx], send_whole.at[dx], recv_whole.at[dx])
-        rows_own += whole[dx]
-    for part in range(2):
-        for k in range(nc):
-            start = part * modes + k * quarter
-            meson_ref[0, :, start : start + quarter] = rows_own[k, part]
-
+    def put_rows():
+        rows_own = piece[x]
+        for dx in range(1, nx):
+            arrived(whole.at[dx], send_whole.at[dx], recv_whole.at[dx])
+            rows_own += whole[dx]
+        for part in range(2):
+            for k in range(nc):
+                start = part * modes + k * quarter
+                meson_ref[0, :, start : start + quarter] = rows_own[k, part]
+
+    table = all_sum(table, sum_y, send_y, recv_y, y, ny, [at(z, y_at(k), x, cut) for k in far_first(ny)], lambda: None)
     table = all_sum(
-        table, sum_x, send_x, recv_x, x * nc + cut, nx * nc, [at(z, y, xx, cc) for xx, cc, _, _ in others]
+        table, sum_x, send_x, recv_x, x * nc + cut, nx * nc, [at(z, y, xx, cc) for xx, cc, _, _ in others], lambda: None
     )
-    table = all_sum(table, sum_z, send_z, recv_z, z, nz, [at(z_at(k), y, x, cut) for k in far_first(nz)])
+    table = all_sum(table, sum_z, send_z, recv_z, z, nz, [at(z_at(k), y, x, cut) for k in far_first(nz)], put_rows)
 
     for part in range(2):
         value = jnp.where(pick[0], table[2 * part : 2 * part + 1], 0.0) + jnp.where(
@@ -444,6 +474,8 @@
 
     for copy in sends:
         copy.wait_send()
+    for quarter_id, copy in quarters:
+        pl.when(cut != quarter_id)(copy.wait_send)
 
 
 def per_device(vectors, momenta, diagrams):

time: 85.8 us -> 85.4 us (level)
  no operation moved by 1% of the time
where the time goes in v5:
time: 85.4 us; the launch traced here: 85.2 us
  Pallas kernels  83.4 us (98%)
  local copies, waits for them, and re-layouts  1.18 us (1%)
    pallas_call x1, Pallas kernels, per_device(): pl.pallas_call(kernel, out_shape=(pltpu.VMEM((1, rows_y // nx, 2 * modes)...  83.4 us

profile of v5, /device:TPU:1, one launch (start us, length us, event | category | flops | bytes accessed | tf_op | source)
XLA Modules:
  0.0 85.2 jit_solution(12824359698856496121)
XLA Ops:
  0.6 83.4 %shard_map.50 = (f32[1,8,1024]{2,1,0:T(8,128)S(1)}, f32[2,64]{1,0:T(2,128)S(1)}) custom-call(f32[1,2,512,256]{3,2,1,0:T(8,128)} %vec_hbm.1, s32[3,3]{1,0:T(4,128)} %mom_ref.1, s32[5,64]{1,0:T(8,128)} %bitcast.3), custom_call_target="tpu_custom_call" | custom-call | tf_op jit(solution)/shard_map/pallas_call | solution.py:534
  84.1 0.6 copy.7
  84.7 0.6 copy.8
